TPU v7x, 512 devices: a whole 4x8x8 slice. The times are simulated.
512 devices in a mesh: row: 32 (over y, z_lo), col: 16 (over z_hi, x, core).
Axes of the slice: x: 4, y: 8, z: 8 (z_hi: 2, z_lo: 4; z = z_hi * 4 + z_lo), core: 2. Of those that a mesh axis runs over, the one named last changes fastest.
Arguments:
- table: float32 [16, 256, 256], P('col', 'row'), may hold values from -4 to 4
- marginals: int32 [4096], replicated, may hold values from 64 to 4095
- visits: int32 [32, 16, 16], P('row', 'col'), may hold values from 0 to 15
- counts: int32 [32, 16, 16, 256, 256], P('row', 'col'), may hold values from 0 to 16, as said below
Outputs:
- gradient: float32 [16, 256, 256], P('col')
Inputs may be any that keep to these rules, and one draw needn't show every extreme that they name: `counts`: about half of the cells of every tile are zero.
All inputs are finite; a program needn't handle non-finite values.
Results may differ from a plain program's by a relative error of at most 0.0031.
Values may be sent and summed in bfloat16 or wider, within the bound.
A program may use at most 128 MiB of HBM per device.

v0:
```python
import jax
import jax.numpy as jnp
from jax import lax
from jax.sharding import PartitionSpec as P

K = 16


LOSS_SCALE = 0.0625


def from_root(value, axis, source):
    kept = jnp.where(lax.axis_index(axis) == source, value, 0).astype(value.dtype)
    return lax.psum(kept, axis)


def tile_terms(row_vectors, col_vectors, count_tile, log_rows, log_cols, log_total):
    logits = lax.dot_general(
        row_vectors, col_vectors, (((1,), (1,)), ((), ())), preferred_element_type=jnp.float32
    )
    count_vals = count_tile.astype(jnp.float32)
    baseline = log_total - log_rows[:, None] - log_cols[None, :]
    margin = logits - baseline
    fitted = (0.1 + 0.25 * jnp.sqrt(count_vals)) * (margin - jnp.log(jnp.maximum(count_vals, 1.0)))
    soft_hinge = jax.nn.sigmoid(margin)
    grad_logits = (jnp.where(count_vals > 0, fitted, soft_hinge) * LOSS_SCALE).astype(jnp.bfloat16)
    row_term = jnp.dot(grad_logits, col_vectors, preferred_element_type=jnp.float32)
    col_term = lax.dot_general(
        grad_logits, row_vectors, (((0,), (0,)), ((), ())), preferred_element_type=jnp.float32
    )
    return (row_term, col_term)


def local(table, marginals, visits, counts):
    blocks = lax.axis_size("col")
    row_devices = lax.axis_size("row")
    own_block = lax.axis_index("row") % blocks
    pieces = table.astype(jnp.bfloat16)
    block_rows = pieces.shape[1] * row_devices
    embed_width = pieces.shape[2]
    log_marg = jnp.log(marginals.astype(jnp.float32)).reshape(blocks, block_rows)
    log_total = jnp.log(jnp.sum(marginals).astype(jnp.float32))
    visited = visits[0, 0]
    count_tiles = counts[0, 0]
    log_rows = log_marg[own_block]
    zero_block = jnp.zeros((block_rows, embed_width), jnp.float32)
    col_block = lax.all_gather(pieces, "row", axis=1, tiled=True)
    row_vectors = from_root(col_block, "col", own_block)[0]
    start_terms = jnp.zeros((K, block_rows, embed_width), jnp.float32)
    shards = lax.all_gather(col_block, "col", axis=0, tiled=True)
    visit_row_sum = zero_block
    visit_col_terms = start_terms
    for k in range(K):
        visit_id = visited[k]
        inside = (visit_id >= 0) & (visit_id < shards.shape[0])
        col_vectors = lax.dynamic_index_in_dim(
            shards, jnp.clip(visit_id, 0, shards.shape[0] - 1), 0, keepdims=False
        )

        def compute(vectors, tile_k=count_tiles[k], log_cols=log_marg[visit_id]):
            return tile_terms(row_vectors, vectors, tile_k, log_rows, log_cols, log_total)

        def skipped(vectors):
            return (zero_block, zero_block)

        row_term, col_term = lax.cond(inside, compute, skipped, col_vectors)
        visit_row_sum = visit_row_sum + row_term
        visit_col_terms = visit_col_terms.at[k].add(col_term)
    block_ids = jnp.arange(1 * lax.axis_size("col"), dtype=jnp.int32)
    result = jnp.zeros((1 * lax.axis_size("col"), block_rows, embed_width), jnp.float32)
    for dense_k in range(K):
        result = result + jnp.where(
            (block_ids == visited[dense_k])[:, None, None], visit_col_terms[dense_k][None], 0.0
        )
    result = result + jnp.where((block_ids == own_block)[:, None, None], visit_row_sum[None], 0.0)
    summed = lax.psum_scatter(result, "col", scatter_dimension=0, tiled=True)
    return lax.psum(summed, "row")


def solution(mesh):
    return jax.shard_map(
        local,
        mesh=mesh,
        in_specs=(
            P("col", "row", None),
            P(),
            P("row", "col", None),
            P("row", "col", None, None, None),
        ),
        out_specs=P("col", None, None),
        check_vma=False,
    )
```

profile of v0, /device:TPU:2, one launch (start us, length us, event | category | flops | bytes accessed | tf_op | source)
XLA Modules:
  0.0 988.8 jit_solution(14721961554316318443)
XLA Ops:
  7.2 82.3 %all_gather.6 = bf16[1,256,256]{2,1,0:T(8,128)(2,1)S(1)} all-gather(bf16[1,8,256]{2,1,0:T(8,128)(2,1)S(1)} %convert_element_type.204), channel_id=1, replica_groups=mesh['row'=32,'col'=16] {'row'}, dimensions={1}, use_global_device_ids=true | all-gather | bytes 135168 | tf_op jit(solution)/shard_map/all_gather | solution.py:47
  130.1 135.8 %all-reduce.4.cloned.1.call-done = bf16[256,256]{1,0:T(8,128)(2,1)} async-done(((bf16[256,256]{1,0:T(8,128)(2,1)}), bf16[256,256]{1,0:T(8,128)(2,1)}) %all-reduce.4.cloned.1.call-update) | async-done | bytes 131088 | tf_op jit(solution)/shard_map/psum | solution.py:14
  265.9 79.2 %all-gather.2.cloned.1.call-done = bf16[16,256,256]{2,1,0:T(8,128)(2,1)} async-done(((bf16[1,256,256]{2,1,0:T(8,128)(2,1)}), bf16[16,256,256]{2,1,0:T(8,128)(2,1)}) %all-gather.2.cloned.1.call-update) | async-done | bytes 2097168 | tf_op jit(solution)/shard_map/all_gather | solution.py:50
  345.1 13.3 %conditional.16 = (f32[256,256]{1,0:T(8,128)S(1)}, f32[16,256,256]{2,1,0:T(8,128)}) conditional(s32[]{:T(128)} %convert_element_type.203, () %tuple.261, (s32[1,1,16,256,256]{4,3,2,1,0:T(8,128)}, s32[]{:T(128)}, bf16[16,256,256]{2,1,0:T(8,128)(2,1)}, bf16[256,256]{1,0:T(8,128)(2,1)}, f32[]{:T(128)}, /*index=5*/f32[1,256]{1,0:T(1,128)S(1)}, ...), branch_computations={%region_2.3_spmd, %region_3.4_spmd} | conditional | flops 101646592 | bytes 15079546 | solution.py:66
  347.8 5.4 copy.21
  358.4 10.6 %conditional.17 = (f32[256,256]{1,0:T(8,128)S(1)}, f32[1,256,256]{2,1,0:T(8,128)S(1)}) conditional(s32[]{:T(128)} %convert_element_type.207, () %tuple.263, (s32[1,1,16,256,256]{4,3,2,1,0:T(8,128)}, s32[]{:T(128)}, bf16[16,256,256]{2,1,0:T(8,128)(2,1)}, bf16[256,256]{1,0:T(8,128)(2,1)}, f32[]{:T(128)}, /*index=5*/f32[1,256]{1,0:T(1,128)S(1)}, ...), branch_computations={%region_4.5_spmd, %region_5.6_spmd} | conditional | flops 101646592 | bytes 10623094 | solution.py:66
  360.9 5.4 copy.22
  369.8 10.9 %conditional.18 = (f32[256,256]{1,0:T(8,128)S(1)}, f32[1,256,256]{2,1,0:T(8,128)S(1)}) conditional(s32[]{:T(128)} %convert_element_type.208, () %tuple.265, (s32[1,1,16,256,256]{4,3,2,1,0:T(8,128)}, s32[]{:T(128)}, bf16[16,256,256]{2,1,0:T(8,128)(2,1)}, bf16[256,256]{1,0:T(8,128)(2,1)}, f32[]{:T(128)}, /*index=5*/f32[1,256]{1,0:T(1,128)S(1)}, ...), branch_computations={%region_6.7_spmd, %region_7.8_spmd} | conditional | flops 101646592 | bytes 10623094 | solution.py:66
  372.5 5.4 copy.23
  382.4 10.6 %conditional.19 = (f32[256,256]{1,0:T(8,128)S(1)}, f32[1,256,256]{2,1,0:T(8,128)S(1)}) conditional(s32[]{:T(128)} %convert_element_type.209, () %tuple.267, (s32[1,1,16,256,256]{4,3,2,1,0:T(8,128)}, s32[]{:T(128)}, bf16[16,256,256]{2,1,0:T(8,128)(2,1)}, bf16[256,256]{1,0:T(8,128)(2,1)}, f32[]{:T(128)}, /*index=5*/f32[1,256]{1,0:T(1,128)S(1)}, ...), branch_computations={%region_8.9_spmd, %region_9.10_spmd} | conditional | flops 101646592 | bytes 10623094 | solution.py:66
  384.9 5.4 copy.24
  394.7 10.6 %conditional.20 = (f32[256,256]{1,0:T(8,128)S(1)}, f32[1,256,256]{2,1,0:T(8,128)S(1)}) conditional(s32[]{:T(128)} %convert_element_type.210, () %tuple.269, (s32[1,1,16,256,256]{4,3,2,1,0:T(8,128)}, s32[]{:T(128)}, bf16[16,256,256]{2,1,0:T(8,128)(2,1)}, bf16[256,256]{1,0:T(8,128)(2,1)}, f32[]{:T(128)}, /*index=5*/f32[1,256]{1,0:T(1,128)S(1)}, ...), branch_computations={%region_10.11_spmd, %region_11.12_spmd} | conditional | flops 101646592 | bytes 10623094 | solution.py:66
  397.2 5.4 copy.25
  407.0 10.4 %conditional.21 = (f32[256,256]{1,0:T(8,128)S(1)}, f32[1,256,256]{2,1,0:T(8,128)S(1)}) conditional(s32[]{:T(128)} %convert_element_type.211, () %tuple.271, (s32[1,1,16,256,256]{4,3,2,1,0:T(8,128)}, s32[]{:T(128)}, bf16[16,256,256]{2,1,0:T(8,128)(2,1)}, bf16[256,256]{1,0:T(8,128)(2,1)}, f32[]{:T(128)}, /*index=5*/f32[1,256]{1,0:T(1,128)S(1)}, ...), branch_computations={%region_12.13_spmd, %region_13.14_spmd} | conditional | flops 101646592 | bytes 10623094 | solution.py:66
  409.3 5.4 copy.26
  419.1 10.4 %conditional.22 = (f32[256,256]{1,0:T(8,128)S(1)}, f32[1,256,256]{2,1,0:T(8,128)S(1)}) conditional(s32[]{:T(128)} %convert_element_type.212, () %tuple.273, (s32[1,1,16,256,256]{4,3,2,1,0:T(8,128)}, s32[]{:T(128)}, bf16[16,256,256]{2,1,0:T(8,128)(2,1)}, bf16[256,256]{1,0:T(8,128)(2,1)}, f32[]{:T(128)}, /*index=5*/f32[1,256]{1,0:T(1,128)S(1)}, ...), branch_computations={%region_14.15_spmd, %region_15.16_spmd} | conditional | flops 101646592 | bytes 10623094 | solution.py:66
  421.4 5.4 copy.27
  431.2 10.4 %conditional.23 = (f32[256,256]{1,0:T(8,128)S(1)}, f32[1,256,256]{2,1,0:T(8,128)S(1)}) conditional(s32[]{:T(128)} %convert_element_type.213, () %tuple.275, (s32[1,1,16,256,256]{4,3,2,1,0:T(8,128)}, s32[]{:T(128)}, bf16[16,256,256]{2,1,0:T(8,128)(2,1)}, bf16[256,256]{1,0:T(8,128)(2,1)}, f32[]{:T(128)}, /*index=5*/f32[1,256]{1,0:T(1,128)S(1)}, ...), branch_computations={%region_16.17_spmd, %region_17.18_spmd} | conditional | flops 101646592 | bytes 10623094 | solution.py:66
  433.5 5.4 copy.28
  443.3 10.8 %conditional.24 = (f32[256,256]{1,0:T(8,128)S(1)}, f32[1,256,256]{2,1,0:T(8,128)S(1)}) conditional(s32[]{:T(128)} %convert_element_type.214, () %tuple.277, (s32[1,1,16,256,256]{4,3,2,1,0:T(8,128)}, s32[]{:T(128)}, bf16[16,256,256]{2,1,0:T(8,128)(2,1)}, bf16[256,256]{1,0:T(8,128)(2,1)}, f32[]{:T(128)}, /*index=5*/f32[1,256]{1,0:T(1,128)S(1)}, ...), branch_computations={%region_18.19_spmd, %region_19.20_spmd} | conditional | flops 101646592 | bytes 10623094 | solution.py:66
  446.0 5.4 copy.29
  455.8 10.6 %conditional.25 = (f32[256,256]{1,0:T(8,128)S(1)}, f32[1,256,256]{2,1,0:T(8,128)S(1)}) conditional(s32[]{:T(128)} %convert_element_type.215, () %tuple.279, (s32[1,1,16,256,256]{4,3,2,1,0:T(8,128)}, s32[]{:T(128)}, bf16[16,256,256]{2,1,0:T(8,128)(2,1)}, bf16[256,256]{1,0:T(8,128)(2,1)}, f32[]{:T(128)}, /*index=5*/f32[1,256]{1,0:T(1,128)S(1)}, ...), branch_computations={%region_20.21_spmd, %region_21.22_spmd} | conditional | flops 101646592 | bytes 10623094 | solution.py:66
  468.2 10.5 %conditional.26 = (f32[256,256]{1,0:T(8,128)S(1)}, f32[1,256,256]{2,1,0:T(8,128)S(1)}) conditional(s32[]{:T(128)} %convert_element_type.216, () %tuple.281, (s32[1,1,16,256,256]{4,3,2,1,0:T(8,128)}, s32[]{:T(128)}, bf16[16,256,256]{2,1,0:T(8,128)(2,1)}, bf16[256,256]{1,0:T(8,128)(2,1)}, f32[]{:T(128)}, /*index=5*/f32[1,256]{1,0:T(1,128)S(1)}, ...), branch_computations={%region_22.23_spmd, %region_23.24_spmd} | conditional | flops 101646592 | bytes 10623094 | solution.py:66
  480.3 10.9 %conditional.27 = (f32[256,256]{1,0:T(8,128)S(1)}, f32[1,256,256]{2,1,0:T(8,128)S(1)}) conditional(s32[]{:T(128)} %convert_element_type.217, () %tuple.283, (s32[1,1,16,256,256]{4,3,2,1,0:T(8,128)}, s32[]{:T(128)}, bf16[16,256,256]{2,1,0:T(8,128)(2,1)}, bf16[256,256]{1,0:T(8,128)(2,1)}, f32[]{:T(128)}, /*index=5*/f32[1,256]{1,0:T(1,128)S(1)}, ...), branch_computations={%region_24.25_spmd, %region_25.26_spmd} | conditional | flops 101646592 | bytes 10623094 | solution.py:66
  493.0 12.3 %conditional.28 = (f32[256,256]{1,0:T(8,128)S(1)}, f32[1,256,256]{2,1,0:T(8,128)}) conditional(s32[]{:T(128)} %convert_element_type.218, () %tuple.285, (s32[1,1,16,256,256]{4,3,2,1,0:T(8,128)}, s32[]{:T(128)}, bf16[16,256,256]{2,1,0:T(8,128)(2,1)}, bf16[256,256]{1,0:T(8,128)(2,1)}, f32[]{:T(128)}, /*index=5*/f32[1,256]{1,0:T(1,128)S(1)}, ...), branch_computations={%region_26.27_spmd, %region_27.28_spmd} | conditional | flops 101646592 | bytes 10623094 | solution.py:66
  507.1 13.3 %conditional.29 = (f32[256,256]{1,0:T(8,128)}, f32[1,256,256]{2,1,0:T(8,128)}) conditional(s32[]{:T(128)} %convert_element_type.219, () %tuple.287, (s32[1,1,16,256,256]{4,3,2,1,0:T(8,128)}, s32[]{:T(128)}, bf16[16,256,256]{2,1,0:T(8,128)(2,1)}, bf16[256,256]{1,0:T(8,128)(2,1)}, f32[]{:T(128)}, /*index=5*/f32[1,256]{1,0:T(1,128)S(1)}, ...), branch_computations={%region_28.29_spmd, %region_29.30_spmd} | conditional | flops 101646592 | bytes 10623094 | solution.py:66
  520.5 13.3 %conditional.30 = (f32[256,256]{1,0:T(8,128)}, f32[1,256,256]{2,1,0:T(8,128)}) conditional(s32[]{:T(128)} %convert_element_type.220, () %tuple.289, (s32[1,1,16,256,256]{4,3,2,1,0:T(8,128)}, s32[]{:T(128)}, bf16[16,256,256]{2,1,0:T(8,128)(2,1)}, bf16[256,256]{1,0:T(8,128)(2,1)}, f32[]{:T(128)}, /*index=5*/f32[1,256]{1,0:T(1,128)S(1)}, ...), branch_computations={%region_30.31_spmd, %region_31.32_spmd} | conditional | flops 101646592 | bytes 10623094 | solution.py:66
  533.8 11.7 %conditional.31 = (f32[256,256]{1,0:T(8,128)S(1)}, f32[1,256,256]{2,1,0:T(8,128)S(1)}) conditional(s32[]{:T(128)} %convert_element_type.221, () %tuple.291, (s32[1,1,16,256,256]{4,3,2,1,0:T(8,128)}, s32[]{:T(128)}, bf16[16,256,256]{2,1,0:T(8,128)(2,1)}, bf16[256,256]{1,0:T(8,128)(2,1)}, f32[]{:T(128)}, /*index=5*/f32[1,256]{1,0:T(1,128)S(1)}, ...), branch_computations={%region_32.33_spmd, %region_33.34_spmd} | conditional | flops 101646592 | bytes 10627218 | solution.py:66
  537.4 5.4 copy.36
  550.7 11.3 %select_add_fusion = f32[16,256,256]{2,1,0:T(8,128)} fusion(f32[256,256]{1,0:T(8,128)S(1)} %add_add_fusion, f32[256,256]{1,0:T(8,128)S(1)} %get-tuple-element.1640, f32[256,256]{1,0:T(8,128)S(1)} %get-tuple-element.1641, f32[256,256]{1,0:T(8,128)S(1)} %get-tuple-element.1642, f32[256,256]{1,0:T(8,128)S(1)} %copy-done.20, ...), kind=kLoop, calls=%fused_computation.288 | loop fusion | flops 34603008 | bytes 8651024 | tf_op jit(solution)/shard_map/add | solution.py:75
  562.1 109.4 %reduce-scatter.2.cloned.1.call-done = f32[1,256,256]{2,1,0:T(8,128)} async-done(((f32[16,256,256]{2,1,0:T(8,128)}), f32[1,256,256]{2,1,0:T(8,128)}) %reduce-scatter.2.cloned.1.call-update) | async-done | bytes 262160 | tf_op jit(solution)/shard_map/reduce_scatter | solution.py:76
  671.6 309.0 %all-reduce.6.cloned.1.call-done = f32[1,256,256]{2,1,0:T(8,128)} async-done(((f32[1,256,256]{2,1,0:T(8,128)}), f32[1,256,256]{2,1,0:T(8,128)}) %all-reduce.6.cloned.1.call-update) | async-done | bytes 262160 | tf_op jit(solution)/shard_map/psum | solution.py:77
  (184 shorter events, 132.9 us)
Async XLA Ops:
  6.5 259.4 %all-reduce.4.cloned.1.call-start = ((), (), s32[]{:S(2)}) async-start(), calls=%async_computation.2 | async-start | bytes 262144 | tf_op jit(solution)/shard_map/psum | solution.py:14
  90.3 254.8 %all-gather.2.cloned.1.call-start = ((), (), s32[]{:S(2)}) async-start(), calls=%async_computation.1 | async-start | bytes 2228224 | tf_op jit(solution)/shard_map/all_gather | solution.py:50
  91.0 580.5 %reduce-scatter.2.cloned.1.call-start = ((), (), s32[]{:S(2)}) async-start(), calls=%async_computation.3 | async-start | bytes 4456448 | tf_op jit(solution)/shard_map/reduce_scatter | solution.py:76
  115.1 365.3 %copy-start.21 = (f32[16,256]{1,0:T(8,128)}, f32[16,256]{1,0:T(8,128)S(1)}, u32[]{:S(2)}) copy-start(f32[16,256]{1,0:T(8,128)S(1)} %reshape.989) | copy-start | bytes 49156
  347.8 5.4 copy-start
  360.9 5.4 copy-start.1
  372.5 5.4 copy-start.2
  384.9 5.4 copy-start.3
  397.2 5.4 copy-start.4
  409.3 5.4 copy-start.5
  421.4 5.4 copy-start.6
  433.5 5.4 copy-start.7
  446.0 5.4 copy-start.8
  458.3 5.4 copy-start.9
  470.5 5.4 copy-start.10
  483.1 5.4 copy-start.11
  496.4 5.4 copy-start.12
  511.0 5.4 copy-start.13
  524.2 5.4 copy-start.14
  537.3 5.5 copy-start.15
  537.3 5.5 copy-start.35
  546.3 3.0 copy-start.18
  549.1 1.5 copy-start.20
  549.1 1.5 copy-start.22
  549.1 1.5 copy-start.23
  549.1 1.5 copy-start.24
  549.2 1.5 copy-start.25
  549.2 1.5 copy-start.26
  549.2 1.5 copy-start.27
  549.2 1.5 copy-start.28
  549.2 1.5 copy-start.29
  562.1 418.5 %all-reduce.6.cloned.1.call-start = ((), (), s32[]{:S(2)}) async-start(), calls=%async_computation.4 | async-start | bytes 524288 | tf_op jit(solution)/shard_map/psum | solution.py:77
  (9 other events, 11.1 us)
Sparse Core Ops, SparseCore 0:
  90.4 175.4 all-reduce.3
  269.2 75.8 all-gather.1
  562.2 109.3 reduce-scatter.1
  674.3 306.2 all-reduce.5
where the time goes:
time: 992 us; the launch traced here: 989 us
  waiting for transfers between devices  634 us (64%)
  local copies, waits for them, and re-layouts  94.5 us (10%)
  blocking collectives  82.3 us (8%)
  other arithmetic  56.7 us (6%)
  matrix products  46.3 us (5%)
  loops' own time  40.4 us (4%)
  between operations  34.2 us (3%)
    psum x1, waiting for transfers between devices, local(): return lax.psum(summed, 'row')  309 us
    psum x1, waiting for transfers between devices, from_root(): return lax.psum(kept, axis)  136 us
    reduce_scatter x1, waiting for transfers between devices, local(): summed = lax.psum_scatter(result, 'col', scatter_dimension=0, tiled=True)  109 us
    another operation x16, local copies, waits for them, and re-layouts  86.8 us
    all_gather x1, blocking collectives, local(): col_block = lax.all_gather(pieces, 'row', axis=1, tiled=True)  82.3 us
    all_gather x1, waiting for transfers between devices, local(): shards = lax.all_gather(col_block, 'col', axis=0, tiled=True)  79.2 us
    another operation x16, loops' own time, local(): row_term, col_term = lax.cond(inside, compute, skipped, col_vectors)  40.4 us
    dot_general x16, matrix products, tile_terms(): lax.dot_general(row_vectors, col_vectors, (((1,), (1,)), ((), ())), prefe...  21.7 us
  transfers between devices with their start and end apart: 4, of which 4 were waited for; matrix products, arithmetic and copies ran while one was open for 2% of the time, Pallas kernels for 0%

commit v1 on v0

v1 whole, which is shorter than its diff:
```python
import jax
import jax.numpy as jnp
from jax import lax
from jax.experimental import pallas as pl
from jax.experimental.pallas import tpu as pltpu
from jax.sharding import PartitionSpec as P

K = 16
MESH = pl.DeviceIdType.MESH
VMEM = pltpu.VMEM
F32 = jnp.float32
BF16 = jnp.bfloat16


def place():
    row = lax.axis_index("row")
    col = lax.axis_index("col")
    y, zl = lax.div(row, 4), lax.rem(row, 4)
    zh, x, core = lax.div(col, 8), lax.rem(lax.div(col, 2), 4), lax.rem(col, 2)
    return y, zl, zh, x, core


def device(y, zl, zh, x, core):
    return (y * 4 + zl, zh * 8 + x * 2 + core)


def partners(y, zl, zh, x, core):
    z = zh * 4 + zl
    found = [device(y, zl, zh, x, 1 - core)]
    for d in range(1, 4):
        found.append(device(y, zl, zh, lax.rem(x + d, 4), core))
    for d in range(1, 8):
        found.append(device(lax.rem(y + d, 8), zl, zh, x, core))
    for d in range(1, 8):
        other = lax.rem(z + d, 8)
        found.append(device(y, lax.rem(other, 4), lax.div(other, 4), x, core))
    return found


def greet(others):
    barrier = pltpu.get_barrier_semaphore()
    for other in others:
        pl.semaphore_signal(barrier, inc=1, device_id=other, device_id_type=MESH)
    pl.semaphore_wait(barrier, len(others))


def push(src, dst, send_sem, recv_sem, target):
    copy = pltpu.make_async_remote_copy(
        src_ref=src,
        dst_ref=dst,
        send_sem=send_sem,
        recv_sem=recv_sem,
        device_id=target,
        device_id_type=MESH,
    )
    copy.start()
    return copy


def arrive(dst, send_sem, recv_sem, target):
    pltpu.make_async_remote_copy(
        src_ref=dst,
        dst_ref=dst,
        send_sem=send_sem,
        recv_sem=recv_sem,
        device_id=target,
        device_id_type=MESH,
    ).wait_recv()


def gather_kernel(piece, full, zbuf, zs, zr, ys, yr, xs, xr, cs, cr):
    y, zl, zh, x, core = place()
    z = zh * 4 + zl
    greet(partners(y, zl, zh, x, core))
    mate = device(y, zl, zh, x, 1 - core)
    sent = []
    for d in (4, 3, 5, 2, 6, 1, 7):
        other = lax.rem(z + d, 8)
        target = device(y, lax.rem(other, 4), lax.div(other, 4), x, core)
        sent.append(push(piece, zbuf.at[z], zs.at[d], zr.at[d], target))
    zbuf[z] = piece[...]
    for d in range(1, 8):
        arrive(zbuf.at[lax.rem(z + 8 - d, 8)], zs.at[d], zr.at[d], mate)
    for h in range(2):
        full[h, x, core, y] = zbuf[h * 4 : h * 4 + 4].reshape(32, 256).astype(BF16)
    mine = full.at[:, x, core, y]
    for d in (4, 3, 5, 2, 6, 1, 7):
        target = device(lax.rem(y + d, 8), zl, zh, x, core)
        sent.append(push(mine, mine, ys.at[d], yr.at[d], target))
    order = (0, 1, 7, 2, 6, 3, 5, 4)
    for d in order:
        held = full.at[:, x, core, lax.rem(y + 8 - d, 8)]
        if d:
            arrive(held, ys.at[d], yr.at[d], mate)
        for e in (2, 1, 3):
            target = device(y, zl, zh, lax.rem(x + e, 4), core)
            sent.append(push(held, held, xs.at[d, e], xr.at[d, e], target))
        sent.append(push(held, held, cs.at[d, 0], cr.at[d, 0], mate))
    for d in order:
        for e in (1, 3, 2):
            held = full.at[:, lax.rem(x + 4 - e, 4), core, lax.rem(y + 8 - d, 8)]
            arrive(held, xs.at[d, e], xr.at[d, e], mate)
            sent.append(push(held, held, cs.at[d, e], cr.at[d, e], mate))
    for d in order:
        for e in range(4):
            held = full.at[:, lax.rem(x + 4 - e, 4), 1 - core, lax.rem(y + 8 - d, 8)]
            arrive(held, cs.at[d, e], cr.at[d, e], mate)
    for copy in sent:
        copy.wait_send()


def tile_kernel(visits, marg, table, counts, own_out, mate_out, log_marg, base, total):
    k = pl.program_id(0)
    own = lax.rem(lax.axis_index("row"), 16)
    core = lax.rem(lax.axis_index("col"), 2)

    @pl.when(k == 0)
    def _():
        log_marg[...] = jnp.log(marg[...].astype(F32))
        all_marg = marg[...]
        summed = jnp.sum(jnp.sum(all_marg, axis=0), axis=1, keepdims=True)
        log_total = jnp.log(summed.astype(F32))
        rows = jnp.broadcast_to(log_marg[own], (256, 256))
        base[...] = log_total - rows.T
        total[...] = jnp.zeros_like(total)

    visit = visits[k]
    row_vectors = table[own]
    col_vectors = table[visit]
    logits = lax.dot_general(
        row_vectors, col_vectors, (((1,), (1,)), ((), ())), preferred_element_type=F32
    )
    n = counts[0].astype(F32)
    margin = logits - (base[...] - log_marg[visit])
    m = jnp.maximum(n, 1.0)
    fitted = (0.1 + 0.25 * (m * lax.rsqrt(m))) * (margin - jnp.log(m))
    hinge = 0.5 * jnp.tanh(0.5 * margin) + 0.5
    g = (jnp.where(n > 0, fitted, hinge) * 0.0625).astype(BF16)
    total[own] += jnp.dot(g, col_vectors, preferred_element_type=F32)
    total[visit] += lax.dot_general(
        g, row_vectors, (((0,), (0,)), ((), ())), preferred_element_type=F32
    )

    @pl.when(k == K - 1)
    def _():
        for j in range(8):
            own_out[j] = total[2 * j + core]
            mate_out[j] = total[2 * j + 1 - core].astype(BF16)


def reduce_kernel(
    own, mate_part, out, cbuf, xout, xin, held, yout, yin, zout, zin,
    cs, cr, xs, xr, ys, yr, zs, zr, ls, lr, gs, gr,
):
    y, zl, zh, x, core = place()
    z = zh * 4 + zl
    greet(partners(y, zl, zh, x, core))
    mate = device(y, zl, zh, x, 1 - core)
    sent = []
    order = (4, 3, 5, 2, 6, 1, 7, 0)
    for d in order:
        q = lax.rem(y + d, 8)
        sent.append(push(mate_part.at[:, :, q], cbuf.at[:, :, q], cs.at[d], cr.at[d], mate))
    for d in order:
        q = lax.rem(y + d, 8)
        arrive(cbuf.at[:, :, q], cs.at[d], cr.at[d], mate)
        for e in (2, 1, 3):
            other = lax.rem(x + e, 4)
            xout[d, e] = (own[:, other, q] + cbuf[:, other, q].astype(F32)).astype(BF16)
            target = device(y, zl, zh, other, core)
            sent.append(push(xout.at[d, e], xin.at[d, e], xs.at[d, e], xr.at[d, e], target))
        held[d] = own[:, x, q] + cbuf[:, x, q].astype(F32)
    for d in order:
        for e in (1, 3, 2):
            arrive(xin.at[d, e], xs.at[d, e], xr.at[d, e], mate)
        part = (
            held[d] + xin[d, 1].astype(F32) + xin[d, 2].astype(F32) + xin[d, 3].astype(F32)
        )
        if d:
            yout[d] = part.astype(BF16)
            target = device(lax.rem(y + d, 8), zl, zh, x, core)
            sent.append(push(yout.at[d], yin.at[d], ys.at[d], yr.at[d], target))
        else:
            summed = part
    for d in (4, 3, 5, 2, 6, 1, 7):
        arrive(yin.at[d], ys.at[d], yr.at[d], mate)
        summed = summed + yin[d].astype(F32)
    zout[...] = summed.reshape(8, 8, 256)
    for d in (4, 3, 5, 2, 6, 1, 7):
        other = lax.rem(z + d, 8)
        target = device(y, lax.rem(other, 4), lax.div(other, 4), x, core)
        sent.append(push(zout.at[other], zin.at[d], zs.at[d], zr.at[d], target))
    last = zout[z]
    for d in (1, 7, 2, 6, 3, 5, 4):
        arrive(zin.at[d], zs.at[d], zr.at[d], mate)
        last = last + zin[d]
    out[y, zl] = last
    mine = out.at[y, zl]
    for e in (1, 2, 3):
        target = device(y, lax.rem(zl + e, 4), zh, x, core)
        sent.append(push(mine, mine, ls.at[e], lr.at[e], target))
    for e in range(4):
        piece = out.at[y, lax.rem(zl + 4 - e, 4)]
        if e:
            arrive(piece, ls.at[e], lr.at[e], mate)
        for d in (4, 3, 5, 2, 6, 1, 7):
            target = device(lax.rem(y + d, 8), zl, zh, x, core)
            sent.append(push(piece, piece, gs.at[e, d], gr.at[e, d], target))
    for e in range(4):
        for d in (1, 7, 2, 6, 3, 5, 4):
            piece = out.at[lax.rem(y + 8 - d, 8), lax.rem(zl + 4 - e, 4)]
            arrive(piece, gs.at[e, d], gr.at[e, d], mate)
    for copy in sent:
        copy.wait_send()


def whole():
    return pl.BlockSpec(memory_space=VMEM)


def local(table, marginals, visits, counts):
    sem = pltpu.SemaphoreType.DMA
    params = pltpu.CompilerParams
    full = pl.pallas_call(
        gather_kernel,
        out_shape=jax.ShapeDtypeStruct((2, 4, 2, 8, 32, 256), BF16),
        in_specs=[whole()],
        out_specs=whole(),
        scratch_shapes=[VMEM((8, 8, 256), F32)]
        + [sem((8,))] * 4
        + [sem((8, 4))] * 4,
        compiler_params=params(collective_id=0, has_side_effects=True),
        name="table_gather",
    )(table[0])
    full = full.reshape(16, 256, 256)
    own, mate_part = pl.pallas_call(
        tile_kernel,
        out_shape=[
            jax.ShapeDtypeStruct((8, 256, 256), F32),
            jax.ShapeDtypeStruct((8, 256, 256), BF16),
        ],
        grid_spec=pltpu.PrefetchScalarGridSpec(
            num_scalar_prefetch=1,
            grid=(K,),
            in_specs=[whole(), whole(), pl.BlockSpec((1, 256, 256), lambda k, v: (k, 0, 0))],
            out_specs=[whole(), whole()],
            scratch_shapes=[
                VMEM((16, 1, 256), F32),
                VMEM((256, 256), F32),
                VMEM((16, 256, 256), F32),
            ],
        ),
        name="tiles",
    )(visits[0, 0], marginals.reshape(16, 1, 256), full, counts[0, 0])
    out = pl.pallas_call(
        reduce_kernel,
        out_shape=jax.ShapeDtypeStruct((8, 4, 8, 256), F32),
        in_specs=[whole(), whole()],
        out_specs=whole(),
        scratch_shapes=[
            VMEM((2, 4, 8, 32, 256), BF16),
            VMEM((8, 4, 2, 32, 256), BF16),
            VMEM((8, 4, 2, 32, 256), BF16),
            VMEM((8, 2, 32, 256), F32),
            VMEM((8, 2, 32, 256), BF16),
            VMEM((8, 2, 32, 256), BF16),
            VMEM((8, 8, 256), F32),
            VMEM((8, 8, 256), F32),
            sem((8,)), sem((8,)),
            sem((8, 4)), sem((8, 4)),
            sem((8,)), sem((8,)),
            sem((8,)), sem((8,)),
            sem((4,)), sem((4,)),
            sem((4, 8)), sem((4, 8)),
        ],
        compiler_params=params(collective_id=1, has_side_effects=True),
        name="gradient_reduce",
    )(own.reshape(2, 4, 8, 32, 256), mate_part.reshape(2, 4, 8, 32, 256))
    return out.reshape(1, 256, 256)


def solution(mesh):
    return jax.shard_map(
        local,
        mesh=mesh,
        in_specs=(
            P("col", "row", None),
            P(),
            P("row", "col", None),
            P("row", "col", None, None, None),
        ),
        out_specs=P("col", None, None),
        check_vma=False,
    )
```

time: 992 us -> 97.9 us (0.10)
  the two profiles are of different devices: /device:TPU:2 before, /device:TPU:8 now
where the time goes in v1:
time: 97.9 us; the launch traced here: 97.4 us
  Pallas kernels  95.7 us (98%)
  local copies, waits for them, and re-layouts  1.67 us (2%)
    pallas_call x1, Pallas kernels, local(): pl.pallas_call(gather_kernel, out_shape=jax.ShapeDtypeStruct((2, 4, 2, 8,...  41.2 us
    pallas_call x1, Pallas kernels, local(): pl.pallas_call(reduce_kernel, out_shape=jax.ShapeDtypeStruct((8, 4, 8, 25...  38.2 us
    pallas_call x1, Pallas kernels, local(): pl.pallas_call(tile_kernel, out_shape=[jax.ShapeDtypeStruct((8, 256, 256)...  16.3 us

profile of v1, /device:TPU:8, one launch (start us, length us, event | category | flops | bytes accessed | tf_op | source)
XLA Modules:
  0.0 97.4 jit_solution(8584320088863371230)
XLA Ops:
  0.0 41.2 %table_gather.1 = bf16[2,4,2,8,32,256]{5,4,3,2,1,0:T(8,128)(2,1)} custom-call(f32[8,256]{1,0:T(8,128)} %bitcast.14), custom_call_target="tpu_custom_call" | custom-call | tf_op jit(solution)/shard_map/table_gather/pallas_call | solution.py:224
  41.2 16.3 %tiles.1 = (f32[8,256,256]{2,1,0:T(8,128)}, bf16[8,256,256]{2,1,0:T(8,128)(2,1)}) custom-call(s32[16]{0:T(128)} %bitcast.15, s32[16,1,256]{2,1,0:T(1,128)} %bitcast.13, bf16[16,256,256]{2,1,0:T(8,128)(2,1)} %bitcast.8, s32[16,256,256]{2,1,0:T(8,128)} %bitcast.9), custom_call_target="tpu_custom_call" | custom-call | tf_op jit(solution)/shard_map/tiles/pallas_call | solution.py:236
  57.5 38.2 %gradient_reduce.1 = f32[8,4,8,256]{3,2,1,0:T(8,128)} custom-call(f32[2,4,8,32,256]{4,3,2,1,0:T(8,128)} %bitcast.10, bf16[2,4,8,32,256]{4,3,2,1,0:T(8,128)(2,1)} %bitcast.11), custom_call_target="tpu_custom_call" | custom-call | tf_op jit(solution)/shard_map/gradient_reduce/pallas_call | solution.py:255
  95.7 1.7 %copy.6 = f32[1,256,256]{2,1,0:T(8,128)} copy(f32[1,256,256]{2,1,0:T(8,128)} %bitcast.12) | data formatting | bytes 524288

commit v2 on v1

--- a/solution.py
+++ b/solution.py
@@ -87,24 +87,54 @@
     for d in (4, 3, 5, 2, 6, 1, 7):
         target = device(lax.rem(y + d, 8), zl, zh, x, core)
         sent.append(push(mine, mine, ys.at[d], yr.at[d], target))
+    right = device(y, zl, zh, lax.rem(x + 1, 4), core)
+    left = device(y, zl, zh, lax.rem(x + 3, 4), core)
     order = (0, 1, 7, 2, 6, 3, 5, 4)
-    for d in order:
-        held = full.at[:, x, core, lax.rem(y + 8 - d, 8)]
+
+    def near(d):
+        from_y = lax.rem(y + 8 - d, 8)
+        held = full.at[:, x, core, from_y]
         if d:
             arrive(held, ys.at[d], yr.at[d], mate)
-        for e in (2, 1, 3):
-            target = device(y, zl, zh, lax.rem(x + e, 4), core)
-            sent.append(push(held, held, xs.at[d, e], xr.at[d, e], target))
+        sent.append(push(held, held, xs.at[d, 0], xr.at[d, 0], right))
+        sent.append(push(held, held, xs.at[d, 1], xr.at[d, 1], left))
         sent.append(push(held, held, cs.at[d, 0], cr.at[d, 0], mate))
+
+    def far(d):
+        from_y = lax.rem(y + 8 - d, 8)
+        before = full.at[:, lax.rem(x + 3, 4), core, from_y]
+        after = full.at[:, lax.rem(x + 1, 4), core, from_y]
+        arrive(before, xs.at[d, 0], xr.at[d, 0], mate)
+        half = full.at[0, lax.rem(x + 3, 4), core, from_y]
+        sent.append(push(half, half, xs.at[d, 2], xr.at[d, 2], right))
+        arrive(after, xs.at[d, 1], xr.at[d, 1], mate)
+        half = full.at[1, lax.rem(x + 1, 4), core, from_y]
+        sent.append(push(half, half, xs.at[d, 3], xr.at[d, 3], left))
+        sent.append(push(before, before, cs.at[d, 1], cr.at[d, 1], mate))
+        sent.append(push(after, after, cs.at[d, 2], cr.at[d, 2], mate))
+
+    def opposite(d):
+        from_y = lax.rem(y + 8 - d, 8)
+        for h in range(2):
+            held = full.at[h, lax.rem(x + 2, 4), core, from_y]
+            arrive(held, xs.at[d, 2 + h], xr.at[d, 2 + h], mate)
+            sent.append(push(held, held, cs.at[d, 3 + h], cr.at[d, 3 + h], mate))
+
+    for step in range(12):
+        if step < 8:
+            near(order[step])
+        if 2 <= step < 10:
+            far(order[step - 2])
+        if step >= 4:
+            opposite(order[step - 4])
     for d in order:
-        for e in (1, 3, 2):
-            held = full.at[:, lax.rem(x + 4 - e, 4), core, lax.rem(y + 8 - d, 8)]
-            arrive(held, xs.at[d, e], xr.at[d, e], mate)
-            sent.append(push(held, held, cs.at[d, e], cr.at[d, e], mate))
-    for d in order:
-        for e in range(4):
-            held = full.at[:, lax.rem(x + 4 - e, 4), 1 - core, lax.rem(y + 8 - d, 8)]
+        from_y = lax.rem(y + 8 - d, 8)
+        for e, source in ((0, x), (1, lax.rem(x + 3, 4)), (2, lax.rem(x + 1, 4))):
+            held = full.at[:, source, 1 - core, from_y]
             arrive(held, cs.at[d, e], cr.at[d, e], mate)
+        for h in range(2):
+            held = full.at[h, lax.rem(x + 2, 4), 1 - core, from_y]
+            arrive(held, cs.at[d, 3 + h], cr.at[d, 3 + h], mate)
     for copy in sent:
         copy.wait_send()
 
@@ -149,67 +179,92 @@
 
 
 def reduce_kernel(
-    own, mate_part, out, cbuf, xout, xin, held, yout, yin, zout, zin,
-    cs, cr, xs, xr, ys, yr, zs, zr, ls, lr, gs, gr,
+    own, mate_part, out, cbuf, xout, xin, kept, held, yout, yin, zout, zin,
+    cs, cr, xs, xr, ys, yr, zs, zr, gs, gr,
 ):
     y, zl, zh, x, core = place()
     z = zh * 4 + zl
     greet(partners(y, zl, zh, x, core))
     mate = device(y, zl, zh, x, 1 - core)
+    right_x, left_x, far_x = lax.rem(x + 1, 4), lax.rem(x + 3, 4), lax.rem(x + 2, 4)
+    right = device(y, zl, zh, right_x, core)
+    left = device(y, zl, zh, left_x, core)
     sent = []
     order = (4, 3, 5, 2, 6, 1, 7, 0)
     for d in order:
         q = lax.rem(y + d, 8)
         sent.append(push(mate_part.at[:, :, q], cbuf.at[:, :, q], cs.at[d], cr.at[d], mate))
-    for d in order:
+
+    def send_x(d, slot, value, target):
+        xout[d, slot] = value.astype(BF16)
+        sent.append(push(xout.at[d, slot], xin.at[d, slot], xs.at[d, slot], xr.at[d, slot], target))
+
+    def wait_x(d, slot):
+        arrive(xin.at[d, slot], xs.at[d, slot], xr.at[d, slot], mate)
+        return xin[d, slot].astype(F32)
+
+    def first(d):
         q = lax.rem(y + d, 8)
         arrive(cbuf.at[:, :, q], cs.at[d], cr.at[d], mate)
-        for e in (2, 1, 3):
-            other = lax.rem(x + e, 4)
-            xout[d, e] = (own[:, other, q] + cbuf[:, other, q].astype(F32)).astype(BF16)
-            target = device(y, zl, zh, other, core)
-            sent.append(push(xout.at[d, e], xin.at[d, e], xs.at[d, e], xr.at[d, e], target))
-        held[d] = own[:, x, q] + cbuf[:, x, q].astype(F32)
-    for d in order:
-        for e in (1, 3, 2):
-            arrive(xin.at[d, e], xs.at[d, e], xr.at[d, e], mate)
-        part = (
-            held[d] + xin[d, 1].astype(F32) + xin[d, 2].astype(F32) + xin[d, 3].astype(F32)
-        )
+
+        def chip(h, block):
+            return own[h, block, q] + cbuf[h, block, q].astype(F32)
+
+        send_x(d, 0, chip(0, far_x), right)
+        send_x(d, 1, chip(1, far_x), left)
+        send_x(d, 2, chip(1, right_x), right)
+        send_x(d, 3, chip(0, left_x), left)
+        kept[d, 0] = chip(0, right_x)
+        kept[d, 1] = chip(1, left_x)
+        held[d, 0] = chip(0, x)
+        held[d, 1] = chip(1, x)
+
+    def second(d):
+        send_x(d, 4, kept[d, 0] + wait_x(d, 0), right)
+        send_x(d, 5, kept[d, 1] + wait_x(d, 1), left)
+
+    def third(d):
+        low = held[d, 0] + wait_x(d, 3) + wait_x(d, 4)
+        high = held[d, 1] + wait_x(d, 2) + wait_x(d, 5)
         if d:
-            yout[d] = part.astype(BF16)
+            yout[d, 0] = low.astype(BF16)
+            yout[d, 1] = high.astype(BF16)
             target = device(lax.rem(y + d, 8), zl, zh, x, core)
             sent.append(push(yout.at[d], yin.at[d], ys.at[d], yr.at[d], target))
         else:
-            summed = part
+            held[d, 0] = low
+            held[d, 1] = high
+
+    for step in range(12):
+        if step < 8:
+            first(order[step])
+        if 2 <= step < 10:
+            second(order[step - 2])
+        if step >= 4:
+            third(order[step - 4])
+    summed = held[0]
     for d in (4, 3, 5, 2, 6, 1, 7):
         arrive(yin.at[d], ys.at[d], yr.at[d], mate)
         summed = summed + yin[d].astype(F32)
-    zout[...] = summed.reshape(8, 8, 256)
+    zout[...] = summed.astype(BF16)
     for d in (4, 3, 5, 2, 6, 1, 7):
         other = lax.rem(z + d, 8)
-        target = device(y, lax.rem(other, 4), lax.div(other, 4), x, core)
-        sent.append(push(zout.at[other], zin.at[d], zs.at[d], zr.at[d], target))
-    last = zout[z]
+        other_h = lax.div(other, 4)
+        target = device(y, lax.rem(other, 4), other_h, x, core)
+        sent.append(push(zout.at[other_h], zin.at[z], zs.at[d], zr.at[d], target))
+    zin[z] = zout[zh]
     for d in (1, 7, 2, 6, 3, 5, 4):
-        arrive(zin.at[d], zs.at[d], zr.at[d], mate)
-        last = last + zin[d]
-    out[y, zl] = last
-    mine = out.at[y, zl]
-    for e in (1, 2, 3):
-        target = device(y, lax.rem(zl + e, 4), zh, x, core)
-        sent.append(push(mine, mine, ls.at[e], lr.at[e], target))
-    for e in range(4):
-        piece = out.at[y, lax.rem(zl + 4 - e, 4)]
-        if e:
-            arrive(piece, ls.at[e], lr.at[e], mate)
-        for d in (4, 3, 5, 2, 6, 1, 7):
-            target = device(lax.rem(y + d, 8), zl, zh, x, core)
-            sent.append(push(piece, piece, gs.at[e, d], gr.at[e, d], target))
-    for e in range(4):
-        for d in (1, 7, 2, 6, 3, 5, 4):
-            piece = out.at[lax.rem(y + 8 - d, 8), lax.rem(zl + 4 - e, 4)]
-            arrive(piece, gs.at[e, d], gr.at[e, d], mate)
+        arrive(zin.at[lax.rem(z + 8 - d, 8)], zs.at[d], zr.at[d], mate)
+    last = zin[0].astype(F32)
+    for source in range(1, 8):
+        last = last + zin[source].astype(F32)
+    out[y] = last.astype(BF16)
+    mine = out.at[y]
+    for d in (4, 3, 5, 2, 6, 1, 7):
+        target = device(lax.rem(y + d, 8), zl, zh, x, core)
+        sent.append(push(mine, mine, gs.at[d], gr.at[d], target))
+    for d in (1, 7, 2, 6, 3, 5, 4):
+        arrive(out.at[lax.rem(y + 8 - d, 8)], gs.at[d], gr.at[d], mate)
     for copy in sent:
         copy.wait_send()
 
@@ -228,7 +283,8 @@
         out_specs=whole(),
         scratch_shapes=[VMEM((8, 8, 256), F32)]
         + [sem((8,))] * 4
-        + [sem((8, 4))] * 4,
+        + [sem((8, 4))] * 2
+        + [sem((8, 5))] * 2,
         compiler_params=params(collective_id=0, has_side_effects=True),
         name="table_gather",
     )(table[0])
@@ -254,29 +310,29 @@
     )(visits[0, 0], marginals.reshape(16, 1, 256), full, counts[0, 0])
     out = pl.pallas_call(
         reduce_kernel,
-        out_shape=jax.ShapeDtypeStruct((8, 4, 8, 256), F32),
+        out_shape=jax.ShapeDtypeStruct((8, 32, 256), BF16),
         in_specs=[whole(), whole()],
         out_specs=whole(),
         scratch_shapes=[
             VMEM((2, 4, 8, 32, 256), BF16),
-            VMEM((8, 4, 2, 32, 256), BF16),
-            VMEM((8, 4, 2, 32, 256), BF16),
+            VMEM((8, 6, 32, 256), BF16),
+            VMEM((8, 6, 32, 256), BF16),
+            VMEM((8, 2, 32, 256), F32),
             VMEM((8, 2, 32, 256), F32),
             VMEM((8, 2, 32, 256), BF16),
             VMEM((8, 2, 32, 256), BF16),
-            VMEM((8, 8, 256), F32),
-            VMEM((8, 8, 256), F32),
+            VMEM((2, 32, 256), BF16),
+            VMEM((8, 32, 256), BF16),
             sem((8,)), sem((8,)),
-            sem((8, 4)), sem((8, 4)),
+            sem((8, 6)), sem((8, 6)),
             sem((8,)), sem((8,)),
             sem((8,)), sem((8,)),
-            sem((4,)), sem((4,)),
-            sem((4, 8)), sem((4, 8)),
+            sem((8,)), sem((8,)),
         ],
         compiler_params=params(collective_id=1, has_side_effects=True),
         name="gradient_reduce",
     )(own.reshape(2, 4, 8, 32, 256), mate_part.reshape(2, 4, 8, 32, 256))
-    return out.reshape(1, 256, 256)
+    return out.reshape(1, 256, 256).astype(F32)
 
 
 def solution(mesh):

time: 97.9 us -> 97.9 us (level)
  the two profiles are of different devices: /device:TPU:8 before, /device:TPU:2 now
where the time goes in v2:
time: 97.9 us; the launch traced here: 97.4 us
  Pallas kernels  95.8 us (98%)
  other arithmetic  1.63 us (2%)
    pallas_call x1, Pallas kernels, local(): pl.pallas_call(gather_kernel, out_shape=jax.ShapeDtypeStruct((2, 4, 2, 8,...  42.9 us
    pallas_call x1, Pallas kernels, local(): pl.pallas_call(reduce_kernel, out_shape=jax.ShapeDtypeStruct((8, 32, 256)...  36.5 us
    pallas_call x1, Pallas kernels, local(): pl.pallas_call(tile_kernel, out_shape=[jax.ShapeDtypeStruct((8, 256, 256)...  16.3 us

profile of v2, /device:TPU:2, one launch (start us, length us, event | category | flops | bytes accessed | tf_op | source)
XLA Modules:
  0.0 97.4 jit_solution(3601046138121535732)
XLA Ops:
  0.0 42.9 %table_gather.1 = bf16[2,4,2,8,32,256]{5,4,3,2,1,0:T(8,128)(2,1)} custom-call(f32[8,256]{1,0:T(8,128)} %bitcast.17), custom_call_target="tpu_custom_call" | custom-call | tf_op jit(solution)/shard_map/table_gather/pallas_call | solution.py:279
  42.9 16.3 %tiles.1 = (f32[8,256,256]{2,1,0:T(8,128)}, bf16[8,256,256]{2,1,0:T(8,128)(2,1)}) custom-call(s32[16]{0:T(128)} %bitcast.18, s32[16,1,256]{2,1,0:T(1,128)} %bitcast.16, bf16[16,256,256]{2,1,0:T(8,128)(2,1)} %bitcast.11, s32[16,256,256]{2,1,0:T(8,128)} %bitcast.12), custom_call_target="tpu_custom_call" | custom-call | tf_op jit(solution)/shard_map/tiles/pallas_call | solution.py:292
  59.2 36.5 %gradient_reduce.1 = bf16[8,32,256]{2,1,0:T(8,128)(2,1)} custom-call(f32[2,4,8,32,256]{4,3,2,1,0:T(8,128)} %bitcast.13, bf16[2,4,8,32,256]{4,3,2,1,0:T(8,128)(2,1)} %bitcast.14), custom_call_target="tpu_custom_call" | custom-call | tf_op jit(solution)/shard_map/gradient_reduce/pallas_call | solution.py:311
  95.8 1.6 %bitcast_convert_fusion = f32[1,256,256]{2,1,0:T(8,128)} fusion(bf16[1,256,256]{2,1,0:T(8,128)(2,1)} %bitcast.15), kind=kLoop, calls=%fused_computation | loop fusion | flops 65536 | bytes 393216 | tf_op jit(solution)/shard_map/convert_element_type | solution.py:335

commit v3 on v2

--- a/solution.py
+++ b/solution.py
@@ -6,6 +6,7 @@
 from jax.sharding import PartitionSpec as P
 
 K = 16
+STEP = 2
 MESH = pl.DeviceIdType.MESH
 VMEM = pltpu.VMEM
 F32 = jnp.float32
@@ -84,9 +85,10 @@
     for h in range(2):
         full[h, x, core, y] = zbuf[h * 4 : h * 4 + 4].reshape(32, 256).astype(BF16)
     mine = full.at[:, x, core, y]
-    for d in (4, 3, 5, 2, 6, 1, 7):
-        target = device(lax.rem(y + d, 8), zl, zh, x, core)
-        sent.append(push(mine, mine, ys.at[d], yr.at[d], target))
+    up = device(lax.rem(y + 1, 8), zl, zh, x, core)
+    down = device(lax.rem(y + 7, 8), zl, zh, x, core)
+    sent.append(push(mine, mine, ys.at[0, 1], yr.at[0, 1], up))
+    sent.append(push(mine, mine, ys.at[1, 1], yr.at[1, 1], down))
     right = device(y, zl, zh, lax.rem(x + 1, 4), core)
     left = device(y, zl, zh, lax.rem(x + 3, 4), core)
     order = (0, 1, 7, 2, 6, 3, 5, 4)
@@ -94,8 +96,15 @@
     def near(d):
         from_y = lax.rem(y + 8 - d, 8)
         held = full.at[:, x, core, from_y]
-        if d:
-            arrive(held, ys.at[d], yr.at[d], mate)
+        if d == 4:
+            arrive(full.at[0, x, core, from_y], ys.at[0, 4], yr.at[0, 4], mate)
+            arrive(full.at[1, x, core, from_y], ys.at[1, 4], yr.at[1, 4], mate)
+        elif d:
+            side, hops = (0, d) if d < 4 else (1, 8 - d)
+            arrive(held, ys.at[side, hops], yr.at[side, hops], mate)
+            part = held if hops < 3 else full.at[side, x, core, from_y]
+            send_sem, recv_sem = ys.at[side, hops + 1], yr.at[side, hops + 1]
+            sent.append(push(part, part, send_sem, recv_sem, (up, down)[side]))
         sent.append(push(held, held, xs.at[d, 0], xr.at[d, 0], right))
         sent.append(push(held, held, xs.at[d, 1], xr.at[d, 1], left))
         sent.append(push(held, held, cs.at[d, 0], cr.at[d, 0], mate))
@@ -154,24 +163,32 @@
         base[...] = log_total - rows.T
         total[...] = jnp.zeros_like(total)
 
-    visit = visits[k]
     row_vectors = table[own]
-    col_vectors = table[visit]
-    logits = lax.dot_general(
-        row_vectors, col_vectors, (((1,), (1,)), ((), ())), preferred_element_type=F32
-    )
-    n = counts[0].astype(F32)
-    margin = logits - (base[...] - log_marg[visit])
-    m = jnp.maximum(n, 1.0)
-    fitted = (0.1 + 0.25 * (m * lax.rsqrt(m))) * (margin - jnp.log(m))
-    hinge = 0.5 * jnp.tanh(0.5 * margin) + 0.5
-    g = (jnp.where(n > 0, fitted, hinge) * 0.0625).astype(BF16)
-    total[own] += jnp.dot(g, col_vectors, preferred_element_type=F32)
-    total[visit] += lax.dot_general(
-        g, row_vectors, (((0,), (0,)), ((), ())), preferred_element_type=F32
-    )
-
-    @pl.when(k == K - 1)
+    terms = []
+    row_term = None
+    for i in range(STEP):
+        visit = visits[k * STEP + i]
+        col_vectors = table[visit]
+        logits = lax.dot_general(
+            row_vectors, col_vectors, (((1,), (1,)), ((), ())), preferred_element_type=F32
+        )
+        n = counts[i].astype(F32)
+        margin = logits - (base[...] - log_marg[visit])
+        m = jnp.maximum(n, 1.0)
+        fitted = (0.1 + 0.25 * (m * lax.rsqrt(m))) * (margin - jnp.log(m))
+        hinge = 0.5 * jnp.tanh(0.5 * margin) + 0.5
+        g = (jnp.where(n > 0, fitted, hinge) * 0.0625).astype(BF16)
+        term = jnp.dot(g, col_vectors, preferred_element_type=F32)
+        row_term = term if row_term is None else row_term + term
+        col_term = lax.dot_general(
+            g, row_vectors, (((0,), (0,)), ((), ())), preferred_element_type=F32
+        )
+        terms.append((visit, col_term))
+    total[own] += row_term
+    for visit, col_term in terms:
+        total[visit] += col_term
+
+    @pl.when(k == K // STEP - 1)
     def _():
         for j in range(8):
             own_out[j] = total[2 * j + core]
@@ -179,11 +196,13 @@
 
 
 def reduce_kernel(
-    own, mate_part, out, cbuf, xout, xin, kept, held, yout, yin, zout, zin,
+    own_hbm, mate_part, out, own, own_sem, cbuf, xout, xin, kept, held, yout, yin, zout, zin,
     cs, cr, xs, xr, ys, yr, zs, zr, gs, gr,
 ):
     y, zl, zh, x, core = place()
     z = zh * 4 + zl
+    fetch = pltpu.make_async_copy(own_hbm, own, own_sem)
+    fetch.start()
     greet(partners(y, zl, zh, x, core))
     mate = device(y, zl, zh, x, 1 - core)
     right_x, left_x, far_x = lax.rem(x + 1, 4), lax.rem(x + 3, 4), lax.rem(x + 2, 4)
@@ -194,6 +213,8 @@
     for d in order:
         q = lax.rem(y + d, 8)
         sent.append(push(mate_part.at[:, :, q], cbuf.at[:, :, q], cs.at[d], cr.at[d], mate))
+
+    fetch.wait()
 
     def send_x(d, slot, value, target):
         xout[d, slot] = value.astype(BF16)
@@ -282,7 +303,8 @@
         in_specs=[whole()],
         out_specs=whole(),
         scratch_shapes=[VMEM((8, 8, 256), F32)]
-        + [sem((8,))] * 4
+        + [sem((8,))] * 2
+        + [sem((2, 5))] * 2
         + [sem((8, 4))] * 2
         + [sem((8, 5))] * 2,
         compiler_params=params(collective_id=0, has_side_effects=True),
@@ -297,8 +319,8 @@
         ],
         grid_spec=pltpu.PrefetchScalarGridSpec(
             num_scalar_prefetch=1,
-            grid=(K,),
-            in_specs=[whole(), whole(), pl.BlockSpec((1, 256, 256), lambda k, v: (k, 0, 0))],
+            grid=(K // STEP,),
+            in_specs=[whole(), whole(), pl.BlockSpec((STEP, 256, 256), lambda k, v: (k, 0, 0))],
             out_specs=[whole(), whole()],
             scratch_shapes=[
                 VMEM((16, 1, 256), F32),
@@ -311,9 +333,11 @@
     out = pl.pallas_call(
         reduce_kernel,
         out_shape=jax.ShapeDtypeStruct((8, 32, 256), BF16),
-        in_specs=[whole(), whole()],
+        in_specs=[pl.BlockSpec(memory_space=pl.ANY)] * 2,
         out_specs=whole(),
         scratch_shapes=[
+            VMEM((2, 4, 8, 32, 256), F32),
+            sem(()),
             VMEM((2, 4, 8, 32, 256), BF16),
             VMEM((8, 6, 32, 256), BF16),
             VMEM((8, 6, 32, 256), BF16),

time: 97.9 us -> 91.5 us (0.935)
  Pallas kernels: 95.8 us -> 89.5 us
    pallas_call x1, Pallas kernels: 16.3 us -> 12.5 us  [local(): pl.pallas_call(tile_kernel, out_shape=[jax.ShapeDtypeStruct((8, 256, 256)...]
    pallas_call x1, Pallas kernels: 36.5 us -> 34.8 us  [local(): pl.pallas_call(reduce_kernel, out_shape=jax.ShapeDtypeStruct((8, 32, 256)...]
where the time goes in v3:
time: 91.5 us; the launch traced here: 91.2 us
  Pallas kernels  89.5 us (98%)
  other arithmetic  1.63 us (2%)
    pallas_call x1, Pallas kernels, local(): pl.pallas_call(gather_kernel, out_shape=jax.ShapeDtypeStruct((2, 4, 2, 8,...  42.2 us
    pallas_call x1, Pallas kernels, local(): pl.pallas_call(reduce_kernel, out_shape=jax.ShapeDtypeStruct((8, 32, 256)...  34.8 us
    pallas_call x1, Pallas kernels, local(): pl.pallas_call(tile_kernel, out_shape=[jax.ShapeDtypeStruct((8, 256, 256)...  12.5 us

profile of v3, /device:TPU:2, one launch (start us, length us, event | category | flops | bytes accessed | tf_op | source)
XLA Modules:
  0.0 91.2 jit_solution(6244869965326723867)
XLA Ops:
  0.0 42.2 %table_gather.1 = bf16[2,4,2,8,32,256]{5,4,3,2,1,0:T(8,128)(2,1)} custom-call(f32[8,256]{1,0:T(8,128)} %bitcast.17), custom_call_target="tpu_custom_call" | custom-call | tf_op jit(solution)/shard_map/table_gather/pallas_call | solution.py:300
  42.2 12.5 %tiles.1 = (f32[8,256,256]{2,1,0:T(8,128)}, bf16[8,256,256]{2,1,0:T(8,128)(2,1)}) custom-call(s32[16]{0:T(128)} %bitcast.18, s32[16,1,256]{2,1,0:T(1,128)} %bitcast.16, bf16[16,256,256]{2,1,0:T(8,128)(2,1)} %bitcast.11, s32[16,256,256]{2,1,0:T(8,128)} %bitcast.12), custom_call_target="tpu_custom_call" | custom-call | tf_op jit(solution)/shard_map/tiles/pallas_call | solution.py:314
  54.7 34.8 %gradient_reduce.1 = bf16[8,32,256]{2,1,0:T(8,128)(2,1)} custom-call(f32[2,4,8,32,256]{4,3,2,1,0:T(8,128)} %bitcast.13, bf16[2,4,8,32,256]{4,3,2,1,0:T(8,128)(2,1)} %bitcast.14), custom_call_target="tpu_custom_call" | custom-call | tf_op jit(solution)/shard_map/gradient_reduce/pallas_call | solution.py:333
  89.5 1.6 %bitcast_convert_fusion = f32[1,256,256]{2,1,0:T(8,128)} fusion(bf16[1,256,256]{2,1,0:T(8,128)(2,1)} %bitcast.15), kind=kLoop, calls=%fused_computation | loop fusion | flops 65536 | bytes 393216 | tf_op jit(solution)/shard_map/convert_element_type | solution.py:359

commit v4 on v3

--- a/solution.py
+++ b/solution.py
@@ -6,7 +6,7 @@
 from jax.sharding import PartitionSpec as P
 
 K = 16
-STEP = 2
+STEP = 4
 MESH = pl.DeviceIdType.MESH
 VMEM = pltpu.VMEM
 F32 = jnp.float32
@@ -87,11 +87,15 @@
     mine = full.at[:, x, core, y]
     up = device(lax.rem(y + 1, 8), zl, zh, x, core)
     down = device(lax.rem(y + 7, 8), zl, zh, x, core)
+    up_two = device(lax.rem(y + 2, 8), zl, zh, x, core)
+    down_two = device(lax.rem(y + 6, 8), zl, zh, x, core)
+    sent.append(push(mine, mine, ys.at[0, 2], yr.at[0, 2], up_two))
+    sent.append(push(mine, mine, ys.at[1, 2], yr.at[1, 2], down_two))
     sent.append(push(mine, mine, ys.at[0, 1], yr.at[0, 1], up))
     sent.append(push(mine, mine, ys.at[1, 1], yr.at[1, 1], down))
     right = device(y, zl, zh, lax.rem(x + 1, 4), core)
     left = device(y, zl, zh, lax.rem(x + 3, 4), core)
-    order = (0, 1, 7, 2, 6, 3, 5, 4)
+    order = (0, 2, 6, 1, 7, 3, 5, 4)
 
     def near(d):
         from_y = lax.rem(y + 8 - d, 8)
@@ -102,9 +106,12 @@
         elif d:
             side, hops = (0, d) if d < 4 else (1, 8 - d)
             arrive(held, ys.at[side, hops], yr.at[side, hops], mate)
-            part = held if hops < 3 else full.at[side, x, core, from_y]
-            send_sem, recv_sem = ys.at[side, hops + 1], yr.at[side, hops + 1]
-            sent.append(push(part, part, send_sem, recv_sem, (up, down)[side]))
+            if hops == 2:
+                half = full.at[side, x, core, from_y]
+                far_target = (up_two, down_two)[side]
+                sent.append(push(half, half, ys.at[side, 4], yr.at[side, 4], far_target))
+                next_target = (up, down)[side]
+                sent.append(push(held, held, ys.at[side, 3], yr.at[side, 3], next_target))
         sent.append(push(held, held, xs.at[d, 0], xr.at[d, 0], right))
         sent.append(push(held, held, xs.at[d, 1], xr.at[d, 1], left))
         sent.append(push(held, held, cs.at[d, 0], cr.at[d, 0], mate))
@@ -129,13 +136,13 @@
             arrive(held, xs.at[d, 2 + h], xr.at[d, 2 + h], mate)
             sent.append(push(held, held, cs.at[d, 3 + h], cr.at[d, 3 + h], mate))
 
-    for step in range(12):
+    for step in range(17):
         if step < 8:
             near(order[step])
-        if 2 <= step < 10:
-            far(order[step - 2])
-        if step >= 4:
-            opposite(order[step - 4])
+        if 5 <= step < 13:
+            far(order[step - 5])
+        if step >= 9:
+            opposite(order[step - 9])
     for d in order:
         from_y = lax.rem(y + 8 - d, 8)
         for e, source in ((0, x), (1, lax.rem(x + 3, 4)), (2, lax.rem(x + 1, 4))):

time: 91.5 us -> 85.2 us (0.931)
  Pallas kernels: 89.5 us -> 83.4 us
    pallas_call x1, Pallas kernels: 42.2 us -> 37.7 us  [local(): pl.pallas_call(gather_kernel, out_shape=jax.ShapeDtypeStruct((2, 4, 2, 8,...]
    pallas_call x1, Pallas kernels: 12.5 us -> 10.9 us  [local(): pl.pallas_call(tile_kernel, out_shape=[jax.ShapeDtypeStruct((8, 256, 256)...]
where the time goes in v4:
time: 85.2 us; the launch traced here: 85 us
  Pallas kernels  83.4 us (98%)
  other arithmetic  1.63 us (2%)
    pallas_call x1, Pallas kernels, local(): pl.pallas_call(gather_kernel, out_shape=jax.ShapeDtypeStruct((2, 4, 2, 8,...  37.7 us
    pallas_call x1, Pallas kernels, local(): pl.pallas_call(reduce_kernel, out_shape=jax.ShapeDtypeStruct((8, 32, 256)...  34.8 us
    pallas_call x1, Pallas kernels, local(): pl.pallas_call(tile_kernel, out_shape=[jax.ShapeDtypeStruct((8, 256, 256)...  10.9 us

profile of v4, /device:TPU:2, one launch (start us, length us, event | category | flops | bytes accessed | tf_op | source)
XLA Modules:
  0.0 85.0 jit_solution(7878452535003654719)
XLA Ops:
  0.0 37.7 %table_gather.1 = bf16[2,4,2,8,32,256]{5,4,3,2,1,0:T(8,128)(2,1)} custom-call(f32[8,256]{1,0:T(8,128)} %bitcast.17), custom_call_target="tpu_custom_call" | custom-call | tf_op jit(solution)/shard_map/table_gather/pallas_call | solution.py:307
  37.7 10.9 %tiles.1 = (f32[8,256,256]{2,1,0:T(8,128)}, bf16[8,256,256]{2,1,0:T(8,128)(2,1)}) custom-call(s32[16]{0:T(128)} %bitcast.18, s32[16,1,256]{2,1,0:T(1,128)} %bitcast.16, bf16[16,256,256]{2,1,0:T(8,128)(2,1)} %bitcast.11, s32[16,256,256]{2,1,0:T(8,128)} %bitcast.12), custom_call_target="tpu_custom_call" | custom-call | tf_op jit(solution)/shard_map/tiles/pallas_call | solution.py:321
  48.5 34.8 %gradient_reduce.1 = bf16[8,32,256]{2,1,0:T(8,128)(2,1)} custom-call(f32[2,4,8,32,256]{4,3,2,1,0:T(8,128)} %bitcast.13, bf16[2,4,8,32,256]{4,3,2,1,0:T(8,128)(2,1)} %bitcast.14), custom_call_target="tpu_custom_call" | custom-call | tf_op jit(solution)/shard_map/gradient_reduce/pallas_call | solution.py:340
  83.4 1.6 %bitcast_convert_fusion = f32[1,256,256]{2,1,0:T(8,128)} fusion(bf16[1,256,256]{2,1,0:T(8,128)(2,1)} %bitcast.15), kind=kLoop, calls=%fused_computation | loop fusion | flops 65536 | bytes 393216 | tf_op jit(solution)/shard_map/convert_element_type | solution.py:366
